TPU v7x, 32 devices: a whole 2x2x4 slice. The times are simulated.
32 devices in a mesh: groups: 2 (over y), seq: 4 (over z), tensor: 2 (over x), sub: 2 (over core).
Axes of the slice: x: 2, y: 2, z: 4, core: 2. Of those that a mesh axis runs over, the one named last changes fastest.
Arguments:
- activations: bfloat16 [4096, 4096], P(('groups', 'seq'), ('tensor', 'sub')), parts along dimension 0, may hold values from -18 to 18
- conv_weight: bfloat16 [512, 4096], P(None, ('tensor', 'sub')), may hold values from -0.25 to 0.25
- query_weight: bfloat16 [4096, 2048], P('seq', ('tensor', 'sub')), may hold values from -0.09375 to 0.09375
- key_weight: bfloat16 [4096, 2048], P('seq', ('tensor', 'sub')), may hold values from -0.09375 to 0.09375
- value_weight: bfloat16 [4096, 2048], P('seq', ('tensor', 'sub')), may hold values from -0.09375 to 0.09375
- segment_for_slot: int32 [16], P('groups'), parts along dimension 0, may hold values from 0 to 7, each once
- book_length: int32 [2], P('groups'), parts along dimension 0, may hold values from 1024 to 2048
Outputs:
- context: bfloat16 [4096, 2048], P(('groups', 'seq'), ('tensor', 'sub')), parts along dimension 0
There are 2 independent parts, one for each index of `groups`. A program takes and returns all parts, laid end to end along the dimension named above; an argument that names none is the same for every part. Nothing has to cross between parts.
Inputs may be any that keep to these rules, and one draw needn't show every extreme that they name: `segment_for_slot`: each segment appears in exactly one slot.
All inputs are finite; a program needn't handle non-finite values.
Results may differ from a plain program's by a relative error of at most 0.012.
The roundings to bfloat16 on the way count: a program that leaves them out, or rounds other values in their place, can miss the bound.
Values may be sent and summed in bfloat16 or wider, within the bound.
No kernel may reach another device: no remote copies, remote signals or barrier semaphores. Data moves between devices by JAX's collectives and lax.ppermute only.
A program may use at most 64 MiB of HBM per device.

v0:
```python
import jax
import jax.numpy as jnp
from jax import lax
from jax.sharding import PartitionSpec as P

HD = 128
CG = 128
RATE = 4
SLOTS = 2
SEG = 256
MEM = 64


def compress_rows(local_rows, conv_local):
    count_rows, channels = local_rows.shape
    groups = channels // CG
    shaped = local_rows.reshape(count_rows // RATE, RATE, groups, CG)
    kernel = conv_local.reshape(RATE, CG, groups, CG)
    mixed_out = jnp.einsum("mtgc,tcgo->mgo", shaped, kernel, preferred_element_type=jnp.float32)
    return mixed_out.reshape(count_rows // RATE, channels).astype(jnp.bfloat16)


def add_product(source, weight_rows):
    return jnp.dot(source, weight_rows, preferred_element_type=jnp.float32)


def local_attention(queries, keys_here, values_here):
    total_rows, head_count, head_dim = queries.shape
    slot_count = total_rows // SEG
    shaped_q = queries.reshape(slot_count, SEG, head_count, head_dim)
    shaped_k = keys_here.reshape(slot_count, SEG, head_count, head_dim)
    shaped_v = values_here.reshape(slot_count, SEG, head_count, head_dim)
    scores = jnp.einsum(
        "asnd,atnd->asnt", shaped_q, shaped_k, preferred_element_type=jnp.float32
    ) * HD ** (-0.5)
    causal = jnp.arange(SEG, dtype=jnp.int32)[:, None] >= jnp.arange(SEG, dtype=jnp.int32)[None, :]
    scores = jnp.where(causal[None, :, None, :], scores, -jnp.inf)
    row_best = jnp.max(scores, axis=3)
    weights = jnp.exp(scores - row_best[..., None])
    denominator = jnp.sum(weights, axis=3)
    weighted_numerator = jnp.einsum(
        "asnt,atnd->asnd",
        weights.astype(jnp.bfloat16),
        shaped_v,
        preferred_element_type=jnp.float32,
    )
    return (
        row_best.reshape(total_rows, head_count),
        denominator.reshape(total_rows, head_count),
        weighted_numerator.reshape(total_rows, head_count, head_dim),
    )


def memory_step(state, pieces, queries, row_segment, segment_for_slot):
    keys_in, values_in = pieces
    count_keys = keys_in.shape[0]
    total_rows, head_count, head_dim = queries.shape
    key_slot = jnp.arange(count_keys, dtype=jnp.int32) // MEM
    slot_ids = jnp.arange(segment_for_slot.shape[0], dtype=jnp.int32)
    key_segment = jnp.sum(
        jnp.where(key_slot[:, None] == slot_ids[None, :], segment_for_slot[None, :], 0), axis=1
    )
    row_best, denominator, weighted_numerator = state
    shaped_keys = keys_in.reshape(count_keys, head_count, head_dim)
    shaped_values = values_in.reshape(count_keys, head_count, head_dim)
    scores = jnp.einsum(
        "rnd,knd->rnk", queries, shaped_keys, preferred_element_type=jnp.float32
    ) * HD ** (-0.5)
    allowed = key_segment[None, None, :] < row_segment[:, None, None]
    scores = jnp.where(allowed, scores, -jnp.inf)
    new_best = jnp.maximum(row_best, jnp.max(scores, axis=2))
    weights = jnp.exp(scores - new_best[:, :, None])
    factor = jnp.exp(row_best - new_best)
    denominator = denominator * factor + jnp.sum(weights, axis=2)
    weighted_numerator = weighted_numerator * factor[:, :, None] + jnp.einsum(
        "rnk,knd->rnd",
        weights.astype(jnp.bfloat16),
        shaped_values,
        preferred_element_type=jnp.float32,
    )
    return (new_best, denominator, weighted_numerator)


def on_device(
    activations, conv_weight, query_weight, key_weight, value_weight, segment_for_slot, book_length
):
    compressed_local = compress_rows(activations, conv_weight)
    full_rows, full_compressed = (
        lax.all_gather(activations, ("tensor", "sub"), axis=1, tiled=True),
        lax.all_gather(compressed_local, ("tensor", "sub"), axis=1, tiled=True),
    )
    total_rows = full_rows.shape[0]
    local_width = query_weight.shape[1]
    head_count = local_width // HD
    shard_index = lax.axis_index("seq")
    my_segments = lax.dynamic_slice_in_dim(segment_for_slot, shard_index * SLOTS, SLOTS, 0)
    row_segment = jnp.repeat(my_segments, SEG, total_repeat_length=total_rows)
    query_rows = lax.all_gather(query_weight, "seq", axis=0, tiled=True)
    key_matrix_rows = lax.all_gather(key_weight, "seq", axis=0, tiled=True)
    value_rows = lax.all_gather(value_weight, "seq", axis=0, tiled=True)
    queries = add_product(full_rows, query_rows).astype(jnp.bfloat16)
    keys_here = add_product(full_rows, key_matrix_rows).astype(jnp.bfloat16)
    values_here = add_product(full_rows, value_rows).astype(jnp.bfloat16)
    keys_mem = add_product(full_compressed, key_matrix_rows).astype(jnp.bfloat16)
    values_mem = add_product(full_compressed, value_rows).astype(jnp.bfloat16)
    shaped_q = queries.reshape(total_rows, head_count, HD)
    state = local_attention(
        shaped_q,
        keys_here.reshape(total_rows, head_count, HD),
        values_here.reshape(total_rows, head_count, HD),
    )
    state = memory_step(
        state,
        (
            lax.all_gather(keys_mem, "seq", axis=0, tiled=True),
            lax.all_gather(values_mem, "seq", axis=0, tiled=True),
        ),
        shaped_q,
        row_segment,
        segment_for_slot,
    )
    row_best, denominator, weighted_numerator = state
    result = (weighted_numerator / denominator[:, :, None]).reshape(total_rows, local_width)
    position = row_segment * SEG + jnp.arange(total_rows, dtype=jnp.int32) % SEG
    result = jnp.where((position < book_length[0])[:, None], result, 0.0)
    return result.astype(jnp.bfloat16)


def solution(mesh):
    placed = (
        P(("groups", "seq"), ("tensor", "sub")),
        P(None, ("tensor", "sub")),
        P("seq", ("tensor", "sub")),
        P("seq", ("tensor", "sub")),
        P("seq", ("tensor", "sub")),
        P("groups"),
        P("groups"),
    )
    return jax.shard_map(
        on_device,
        mesh=mesh,
        in_specs=placed,
        out_specs=P(("groups", "seq"), ("tensor", "sub")),
        check_vma=False,
    )
```

profile of v0, /device:TPU:0, one launch (start us, length us, event | category | flops | bytes accessed | tf_op | source)
XLA Modules:
  0.0 350.5 jit_solution(3054702752094949203)
XLA Ops:
  6.5 0.7 all-gather.6.cloned.1.call-update
  7.3 0.7 all-gather.10.cloned.1.call-update
  8.1 0.7 all-gather.12.cloned.1.call-update
  8.8 1.5 copy.64
  10.3 0.3 copy.65
  10.6 1.7 fusion.17
  12.4 0.5 all-gather.8.cloned.1.call-update
  13.6 0.6 fusion.41
  14.3 1.3 fusion.32
  15.6 1.3 broadcast_select_fusion
  16.9 0.2 broadcast_compare_fusion
  17.1 29.0 %all-gather.6.cloned.1.call-done = bf16[512,4096]{1,0:T(8,128)(2,1)} async-done(((bf16[512,1024]{1,0:T(8,128)(2,1)}), bf16[512,4096]{1,0:T(8,128)(2,1)}) %all-gather.6.cloned.1.call-update) | async-done | bytes 4194320 | tf_op jit(solution)/shard_map/all_gather | solution.py:89
  46.1 82.4 %all-gather.10.cloned.1.call-done = bf16[4096,512]{1,0:T(8,128)(2,1)} async-done(((bf16[1024,512]{1,0:T(8,128)(2,1)}), bf16[4096,512]{1,0:T(8,128)(2,1)}) %all-gather.10.cloned.1.call-update) | async-done | bytes 4194320 | tf_op jit(solution)/shard_map/all_gather | solution.py:99
  128.5 5.8 %convolution_convert_fusion.1 = bf16[512,512]{1,0:T(8,128)(2,1)S(1)} fusion(bf16[512,4096]{1,0:T(8,128)(2,1)} %all-gather.6.cloned.1.call-done, bf16[4096,512]{1,0:T(8,128)(2,1)} %all-gather.10.cloned.1.call-done), kind=kOutput, calls=%fused_computation.18 | convolution fusion | flops 2147745792 | bytes 8912896 | tf_op jit(solution)/shard_map/dot_general | solution.py:24
  134.4 75.0 %all-gather.12.cloned.1.call-done = bf16[4096,512]{1,0:T(8,128)(2,1)} async-done(((bf16[1024,512]{1,0:T(8,128)(2,1)}), bf16[4096,512]{1,0:T(8,128)(2,1)}) %all-gather.12.cloned.1.call-update) | async-done | bytes 4194320 | tf_op jit(solution)/shard_map/all_gather | solution.py:98
  209.4 5.8 %convolution_convert_fusion = bf16[512,512]{0,1:T(8,128)(2,1)S(1)} fusion(bf16[512,4096]{1,0:T(8,128)(2,1)} %all-gather.6.cloned.1.call-done, bf16[4096,512]{1,0:T(8,128)(2,1)} %all-gather.12.cloned.1.call-done), kind=kOutput, calls=%fused_computation.17 | convolution fusion | flops 2147745792 | bytes 8912896 | tf_op jit(solution)/shard_map/dot_general | solution.py:24
  215.4 10.7 %all-gather.14.cloned.1.call-done = bf16[128,4096]{0,1:T(8,128)(2,1)} async-done(((bf16[128,1024]{0,1:T(8,128)(2,1)}), bf16[128,4096]{0,1:T(8,128)(2,1)}) %all-gather.14.cloned.1.call-update) | async-done | bytes 1048592 | tf_op jit(solution)/shard_map/all_gather | solution.py:90
  226.1 3.3 convolution_convert_fusion.4
  229.4 21.4 %all_gather.26 = bf16[512,512]{1,0:T(8,128)(2,1)} all-gather(bf16[128,512]{1,0:T(8,128)(2,1)S(1)} %convolution_convert_fusion.4), channel_id=1, replica_groups=mesh['groups'=2,'seq'=4,'tensor'=2,'sub'=2] {'seq'}, dimensions={0}, use_global_device_ids=true | all-gather | bytes 655360 | tf_op jit(solution)/shard_map/all_gather | solution.py:115
  250.8 61.4 %all-gather.8.cloned.1.call-done = bf16[4096,512]{1,0:T(8,128)(2,1)} async-done(((bf16[1024,512]{1,0:T(8,128)(2,1)}), bf16[4096,512]{1,0:T(8,128)(2,1)}) %all-gather.8.cloned.1.call-update) | async-done | bytes 4194320 | tf_op jit(solution)/shard_map/all_gather | solution.py:100
  312.2 5.8 %convolution_convert_fusion.2 = bf16[512,512]{1,0:T(8,128)(2,1)S(1)} fusion(bf16[512,4096]{1,0:T(8,128)(2,1)} %all-gather.6.cloned.1.call-done, bf16[4096,512]{1,0:T(8,128)(2,1)} %all-gather.8.cloned.1.call-done), kind=kOutput, calls=%fused_computation.19 | convolution fusion | flops 2147745792 | bytes 8912896 | tf_op jit(solution)/shard_map/dot_general | solution.py:24
  318.1 0.5 fusion.42
  318.6 0.3 fusion.9
  318.9 0.5 convolution_bitcast_fusion
  319.4 0.3 copy.49
  319.7 0.3 copy.54
  320.1 3.0 convolution_convert_fusion.3
  323.1 15.2 %all_gather.27 = bf16[512,512]{1,0:T(8,128)(2,1)S(1)} all-gather(bf16[128,512]{1,0:T(8,128)(2,1)S(1)} %convolution_convert_fusion.3), channel_id=1, replica_groups=mesh['groups'=2,'seq'=4,'tensor'=2,'sub'=2] {'seq'}, dimensions={0}, use_global_device_ids=true | all-gather | bytes 655360 | tf_op jit(solution)/shard_map/all_gather | solution.py:116
  338.6 1.9 fusion.2
  340.5 0.9 fusion
  341.4 1.4 fusion.22
  343.0 1.0 select_convert_fusion
  (29 shorter events, 1.2 us)
Async XLA Ops:
  6.5 3.8 %copy-start = (bf16[512,1024]{1,0:T(8,128)(2,1)S(1)}, bf16[512,1024]{1,0:T(8,128)(2,1)}, u32[]{:S(2)}) copy-start(bf16[512,1024]{1,0:T(8,128)(2,1)} %param.9) | copy-start | bytes 3145732
  6.5 39.6 %all-gather.6.cloned.1.call-start = ((), (), s32[]{:S(2)}) async-start(), calls=%async_computation | async-start | bytes 5242880 | tf_op jit(solution)/shard_map/all_gather | solution.py:89
  7.3 121.2 %all-gather.10.cloned.1.call-start = ((), (), s32[]{:S(2)}) async-start(), calls=%async_computation.2 | async-start | bytes 5242880 | tf_op jit(solution)/shard_map/all_gather | solution.py:99
  8.0 201.4 %all-gather.12.cloned.1.call-start = ((), (), s32[]{:S(2)}) async-start(), calls=%async_computation.3 | async-start | bytes 5242880 | tf_op jit(solution)/shard_map/all_gather | solution.py:98
  8.7 217.4 %all-gather.14.cloned.1.call-start = ((), (), s32[]{:S(2)}) async-start(), calls=%async_computation.4 | async-start | bytes 1310720 | tf_op jit(solution)/shard_map/all_gather | solution.py:90
  8.8 4.8 %copy-start.5 = (s32[8]{0:T(128)S(1)}, s32[8]{0:T(128)}, u32[]{:S(2)}) copy-start(s32[8]{0:T(128)} %param.14) | copy-start | bytes 100
  8.8 5.5 %copy-start.4 = (pred[512]{0:T(512)(128)(4,1)S(1)}, pred[512]{0:T(512)(128)(4,1)}, u32[]{:S(2)}) copy-start(pred[512]{0:T(512)(128)(4,1)} %constant.157) | copy-start | bytes 1540
  12.3 299.9 %all-gather.8.cloned.1.call-start = ((), (), s32[]{:S(2)}) async-start(), calls=%async_computation.1 | async-start | bytes 5242880 | tf_op jit(solution)/shard_map/all_gather | solution.py:100
  215.2 96.9 %copy-start.3 = (bf16[512,512]{0,1:T(8,128)(2,1)}, bf16[512,512]{0,1:T(8,128)(2,1)S(1)}, u32[]{:S(2)}) copy-start(bf16[512,512]{0,1:T(8,128)(2,1)S(1)} %convolution_convert_fusion) | copy-start | bytes 1572868
  318.9 1.2 copy-start.1
  320.1 18.4 %copy-start.2 = (bf16[512,512]{1,0:T(8,128)(2,1)S(1)}, bf16[512,512]{1,0:T(8,128)(2,1)}, u32[]{:S(2)}) copy-start(bf16[512,512]{1,0:T(8,128)(2,1)} %all_gather.26) | copy-start | bytes 1572868
Sparse Core Ops, SparseCore 0:
  8.9 37.1 all-gather.5
  47.7 80.7 all-gather.9
  130.1 79.2 all-gather.11
  210.8 15.2 all-gather.13
  227.5 84.6 all-gather.7
where the time goes:
time: 351 us
  waiting for transfers between devices  261 us (74%)
  blocking collectives  36.6 us (10%)
  matrix products  29.6 us (8%)
  between operations  14 us (4%)
  other arithmetic  5.11 us (1%)
  local copies, waits for them, and re-layouts  3.95 us (1%)
    all_gather x1, waiting for transfers between devices, on_device(): key_matrix_rows = lax.all_gather(key_weight, 'seq', axis=0, tiled=True)  82.4 us
    all_gather x1, waiting for transfers between devices, on_device(): query_rows = lax.all_gather(query_weight, 'seq', axis=0, tiled=True)  75 us
    all_gather x1, waiting for transfers between devices, on_device(): value_rows = lax.all_gather(value_weight, 'seq', axis=0, tiled=True)  61.4 us
    all_gather x1, waiting for transfers between devices, on_device(): lax.all_gather(activations, ('tensor', 'sub'), axis=1, tiled=True)  29 us
    dot_general x5, matrix products, add_product(): return jnp.dot(source, weight_rows, preferred_element_type=jnp.float32)  23.6 us
    all_gather x1, blocking collectives, on_device(): lax.all_gather(keys_mem, 'seq', axis=0, tiled=True)  21.4 us
    all_gather x1, blocking collectives, on_device(): lax.all_gather(values_mem, 'seq', axis=0, tiled=True)  15.2 us
    all_gather x1, waiting for transfers between devices, on_device(): lax.all_gather(compressed_local, ('tensor', 'sub'), axis=1, tiled=True)  10.7 us
  transfers between devices with their start and end apart: 5, of which 5 were waited for; matrix products, arithmetic and copies ran while one was open for 6% of the time, Pallas kernels for 0%

commit v1 on v0

--- a/solution.py
+++ b/solution.py
@@ -96,7 +96,12 @@
     my_segments = lax.dynamic_slice_in_dim(segment_for_slot, shard_index * SLOTS, SLOTS, 0)
     row_segment = jnp.repeat(my_segments, SEG, total_repeat_length=total_rows)
     query_rows = lax.all_gather(query_weight, "seq", axis=0, tiled=True)
-    key_matrix_rows = lax.all_gather(key_weight, "seq", axis=0, tiled=True)
+    ring = [key_weight]
+    for hop in range(3):
+        ring.append(lax.ppermute(ring[-1], "seq", [(dev, (dev + 1) % 4) for dev in range(4)]))
+    key_matrix_rows = jnp.roll(
+        jnp.concatenate(ring[::-1], axis=0), (lax.axis_index("seq") + 1) * ring[0].shape[0], axis=0
+    )
     value_rows = lax.all_gather(value_weight, "seq", axis=0, tiled=True)
     queries = add_product(full_rows, query_rows).astype(jnp.bfloat16)
     keys_here = add_product(full_rows, key_matrix_rows).astype(jnp.bfloat16)

time: 351 us -> 290 us (0.83)
  waiting for transfers between devices: 261 us -> 179 us
  local copies, waits for them, and re-layouts: 3.95 us -> 16.2 us
  blocking collectives: 36.6 us -> 42.3 us
    ppermute x0 -> x3, waiting for transfers between devices: none -> 86.7 us  [on_device(): lax.ppermute(ring[-1], 'seq', [(dev, (dev + 1) % 4) for dev in range(4)])]
    all_gather x1 -> x0, waiting for transfers between devices: 82.4 us -> none  [on_device(): key_matrix_rows = lax.all_gather(key_weight, 'seq', axis=0, tiled=True)]
    all_gather x1, waiting for transfers between devices: 75 us -> 15.8 us  [on_device(): query_rows = lax.all_gather(query_weight, 'seq', axis=0, tiled=True)]
    all_gather x1, waiting for transfers between devices: 29 us -> 0.01 us  [on_device(): lax.all_gather(activations, ('tensor', 'sub'), axis=1, tiled=True)]
    all_gather x1, waiting for transfers between devices: 61.4 us -> 74.2 us  [on_device(): value_rows = lax.all_gather(value_weight, 'seq', axis=0, tiled=True)]
    unnamed x14 -> x21, local copies, waits for them, and re-layouts: 1.83 us -> 13 us
    all_gather x1, waiting for transfers between devices: 10.7 us -> 0.01 us  [on_device(): lax.all_gather(compressed_local, ('tensor', 'sub'), axis=1, tiled=True)]
    all_gather x1, blocking collectives: 21.4 us -> 26 us  [on_device(): lax.all_gather(keys_mem, 'seq', axis=0, tiled=True)]
  transfers between devices with their start and end apart: 5 -> 7, of which waited for: 5 -> 5; matrix products, arithmetic and copies ran while one was open for 6% -> 10% of each run, Pallas kernels for 0% -> 0%
where the time goes in v1:
time: 290 us; the launch traced here: 289 us
  waiting for transfers between devices  179 us (62%)
  blocking collectives  42.3 us (15%)
  matrix products  29.7 us (10%)
  local copies, waits for them, and re-layouts  16.2 us (6%)
  between operations  14 us (5%)
  other arithmetic  5.07 us (2%)
  starting transfers between devices  3.2 us (1%)
    ppermute x3, waiting for transfers between devices, on_device(): lax.ppermute(ring[-1], 'seq', [(dev, (dev + 1) % 4) for dev in range(4)])  86.7 us
    all_gather x1, waiting for transfers between devices, on_device(): value_rows = lax.all_gather(value_weight, 'seq', axis=0, tiled=True)  74.2 us
    all_gather x1, blocking collectives, on_device(): lax.all_gather(keys_mem, 'seq', axis=0, tiled=True)  26 us
    dot_general x5, matrix products, add_product(): return jnp.dot(source, weight_rows, preferred_element_type=jnp.float32)  23.7 us
    all_gather x1, blocking collectives, on_device(): lax.all_gather(values_mem, 'seq', axis=0, tiled=True)  16.4 us
    all_gather x1, waiting for transfers between devices, on_device(): query_rows = lax.all_gather(query_weight, 'seq', axis=0, tiled=True)  15.8 us
    unnamed x21, local copies, waits for them, and re-layouts  13 us
  transfers between devices with their start and end apart: 7, of which 5 were waited for; matrix products, arithmetic and copies ran while one was open for 10% of the time, Pallas kernels for 0%

profile of v1, /device:TPU:0, one launch (start us, length us, event | category | flops | bytes accessed | tf_op | source)
XLA Modules:
  0.0 289.1 jit_solution(17182461577292243757)
XLA Ops:
  6.5 1.5 copy.64
  8.1 1.6 copy.65
  9.7 1.7 fusion.27
  11.4 0.7 all-gather.5.cloned.1.call-update
  12.1 0.7 all-gather.9.cloned.1.call-update
  13.4 3.1 %collective-permute-start = (bf16[1024,512]{1,0:T(8,128)(2,1)S(1)}, bf16[1024,512]{1,0:T(8,128)(2,1)S(1)}, u32[]{:S(2)}, u32[]{:S(2)}) collective-permute-start(bf16[1024,512]{1,0:T(8,128)(2,1)S(1)} %copy-done), channel_id=1, source_target_pairs={{0,4},{4,8},{8,12},{12,0},{1,5},{5,9},{9,13},{13,1},{2,6},{6,10},{... | collective-permute-start | bytes 3145736 | tf_op jit(solution)/shard_map/ppermute | solution.py:101
  16.5 25.2 %collective-permute-done = bf16[1024,512]{1,0:T(8,128)(2,1)S(1)} collective-permute-done((bf16[1024,512]{1,0:T(8,128)(2,1)S(1)}, bf16[1024,512]{1,0:T(8,128)(2,1)S(1)}, u32[]{:S(2)}, u32[]{:S(2)}) %collective-permute-start) | collective-permute-done | bytes 1048608 | tf_op jit(solution)/shard_map/ppermute | solution.py:101
  41.7 26.1 %collective-permute-done.1 = bf16[1024,512]{1,0:T(8,128)(2,1)S(1)} collective-permute-done((bf16[1024,512]{1,0:T(8,128)(2,1)S(1)}, bf16[1024,512]{1,0:T(8,128)(2,1)S(1)}, u32[]{:S(2)}, u32[]{:S(2)}) %collective-permute-start.1) | collective-permute-done | bytes 1048608 | tf_op jit(solution)/shard_map/ppermute | solution.py:101
  69.3 1.3 fusion.45
  70.6 1.3 broadcast_select_fusion
  72.1 35.3 %collective-permute-done.2 = bf16[1024,512]{1,0:T(8,128)(2,1)} collective-permute-done((bf16[1024,512]{1,0:T(8,128)(2,1)S(1)}, bf16[1024,512]{1,0:T(8,128)(2,1)}, u32[]{:S(2)}, u32[]{:S(2)}) %collective-permute-start.2) | collective-permute-done | bytes 1048608 | tf_op jit(solution)/shard_map/ppermute | solution.py:101
  107.4 2.3 constant_dynamic-update-slice_fusion.7
  109.7 1.1 constant_dynamic-update-slice_fusion.6
  110.8 1.1 constant_dynamic-update-slice_fusion.5
  111.8 1.1 constant_dynamic-update-slice_fusion.4
  112.9 2.3 constant_dynamic-update-slice_fusion.3
  115.1 1.1 constant_dynamic-update-slice_fusion.2
  116.2 1.1 constant_dynamic-update-slice_fusion.1
  117.3 1.1 constant_dynamic-update-slice_fusion
  118.3 3.3 %fusion.28 = bf16[128,512]{1,0:T(8,128)(2,1)S(1)} fusion(bf16[128,4096]{0,1:T(8,128)(2,1)} %all-gather.11.cloned.1.call-done, bf16[8192,512]{1,0:T(8,128)(2,1)} %constant_dynamic-update-slice_fusion, s32[]{:T(128)S(6)} %select_n.84), kind=kOutput, calls=%fused_computation.27 | convolution fusion | flops 536936448 | bytes 5373956 | tf_op jit(solution)/shard_map/dot_general | solution.py:24
  121.6 26.0 %all_gather.22 = bf16[512,512]{1,0:T(8,128)(2,1)} all-gather(bf16[128,512]{1,0:T(8,128)(2,1)S(1)} %fusion.28), channel_id=1, replica_groups=mesh['groups'=2,'seq'=4,'tensor'=2,'sub'=2] {'seq'}, dimensions={0}, use_global_device_ids=true | all-gather | bytes 655360 | tf_op jit(solution)/shard_map/all_gather | solution.py:120
  147.6 5.8 %fusion.24 = bf16[512,512]{0,1:T(8,128)(2,1)S(1)} fusion(bf16[512,4096]{1,0:T(8,128)(2,1)} %all-gather.5.cloned.1.call-done, bf16[8192,512]{1,0:T(8,128)(2,1)} %constant_dynamic-update-slice_fusion, s32[]{:T(128)S(6)} %select_n.84), kind=kOutput, calls=%fused_computation.25 | convolution fusion | flops 2147745792 | bytes 8912900 | tf_op jit(solution)/shard_map/dot_general | solution.py:24
  153.6 15.8 %all-gather.9.cloned.1.call-done = bf16[4096,512]{1,0:T(8,128)(2,1)} async-done(((bf16[1024,512]{1,0:T(8,128)(2,1)}), bf16[4096,512]{1,0:T(8,128)(2,1)}) %all-gather.9.cloned.1.call-update) | async-done | bytes 4194320 | tf_op jit(solution)/shard_map/all_gather | solution.py:98
  169.4 5.8 %convolution_convert_fusion = bf16[512,512]{0,1:T(8,128)(2,1)S(1)} fusion(bf16[512,4096]{1,0:T(8,128)(2,1)} %all-gather.5.cloned.1.call-done, bf16[4096,512]{1,0:T(8,128)(2,1)} %all-gather.9.cloned.1.call-done), kind=kOutput, calls=%fused_computation.22 | convolution fusion | flops 2147745792 | bytes 8912896 | tf_op jit(solution)/shard_map/dot_general | solution.py:24
  175.4 74.2 %all-gather.7.cloned.1.call-done = bf16[4096,512]{1,0:T(8,128)(2,1)} async-done(((bf16[1024,512]{1,0:T(8,128)(2,1)}), bf16[4096,512]{1,0:T(8,128)(2,1)}) %all-gather.7.cloned.1.call-update) | async-done | bytes 4194320 | tf_op jit(solution)/shard_map/all_gather | solution.py:105
  249.6 5.8 %convolution_convert_fusion.1 = bf16[512,512]{1,0:T(8,128)(2,1)S(1)} fusion(bf16[512,4096]{1,0:T(8,128)(2,1)} %all-gather.5.cloned.1.call-done, bf16[4096,512]{1,0:T(8,128)(2,1)} %all-gather.7.cloned.1.call-done), kind=kOutput, calls=%fused_computation.23 | convolution fusion | flops 2147745792 | bytes 8912896 | tf_op jit(solution)/shard_map/dot_general | solution.py:24
  257.6 3.0 %convolution_convert_fusion.2 = bf16[128,512]{1,0:T(8,128)(2,1)S(1)} fusion(bf16[128,4096]{0,1:T(8,128)(2,1)S(1)} %copy-done.1, bf16[4096,512]{1,0:T(8,128)(2,1)} %all-gather.7.cloned.1.call-done), kind=kOutput, calls=%fused_computation.28 | convolution fusion | flops 536936448 | bytes 5373952 | tf_op jit(solution)/shard_map/dot_general | solution.py:24
  260.6 16.4 %all_gather.23 = bf16[512,512]{1,0:T(8,128)(2,1)S(1)} all-gather(bf16[128,512]{1,0:T(8,128)(2,1)S(1)} %convolution_convert_fusion.2), channel_id=1, replica_groups=mesh['groups'=2,'seq'=4,'tensor'=2,'sub'=2] {'seq'}, dimensions={0}, use_global_device_ids=true | all-gather | bytes 655360 | tf_op jit(solution)/shard_map/all_gather | solution.py:121
  277.2 1.9 fusion.6
  279.1 0.9 fusion
  280.0 1.4 fusion.35
  281.6 1.0 select_convert_fusion
  (40 shorter events, 4.6 us)
Async XLA Ops:
  6.5 111.8 %all-gather.11.cloned.1.call-start = ((), (), s32[]{:S(2)}) async-start(), calls=%async_computation.3 | async-start | bytes 1310720 | tf_op jit(solution)/shard_map/all_gather | solution.py:90
  8.0 5.4 %copy-start = (bf16[1024,512]{1,0:T(8,128)(2,1)S(1)}, bf16[1024,512]{1,0:T(8,128)(2,1)}, u32[]{:S(2)}) copy-start(bf16[1024,512]{1,0:T(8,128)(2,1)} %param.12) | copy-start | bytes 3145732
  8.0 60.4 %copy-start.5 = (s32[8]{0:T(128)S(1)}, s32[8]{0:T(128)}, u32[]{:S(2)}) copy-start(s32[8]{0:T(128)} %param.14) | copy-start | bytes 100
  8.1 61.2 %copy-start.4 = (pred[512]{0:T(512)(128)(4,1)S(1)}, pred[512]{0:T(512)(128)(4,1)}, u32[]{:S(2)}) copy-start(pred[512]{0:T(512)(128)(4,1)} %constant.181) | copy-start | bytes 1540
  11.3 136.3 %all-gather.5.cloned.1.call-start = ((), (), s32[]{:S(2)}) async-start(), calls=%async_computation | async-start | bytes 5242880 | tf_op jit(solution)/shard_map/all_gather | solution.py:89
  12.1 157.3 %all-gather.9.cloned.1.call-start = ((), (), s32[]{:S(2)}) async-start(), calls=%async_computation.2 | async-start | bytes 5242880 | tf_op jit(solution)/shard_map/all_gather | solution.py:98
  12.8 236.8 %all-gather.7.cloned.1.call-start = ((), (), s32[]{:S(2)}) async-start(), calls=%async_computation.1 | async-start | bytes 5242880 | tf_op jit(solution)/shard_map/all_gather | solution.py:105
  13.4 28.3 %collective-permute-start = (bf16[1024,512]{1,0:T(8,128)(2,1)S(1)}, bf16[1024,512]{1,0:T(8,128)(2,1)S(1)}, u32[]{:S(2)}, u32[]{:S(2)}) collective-permute-start(bf16[1024,512]{1,0:T(8,128)(2,1)S(1)} %copy-done), channel_id=1, source_target_pairs={{0,4},{4,8},{8,12},{12,0},{1,5},{5,9},{9,13},{13,1},{2,6},{6,10},{... | collective-permute-start | bytes 3145736 | tf_op jit(solution)/shard_map/ppermute | solution.py:101
  41.7 26.1 %collective-permute-start.1 = (bf16[1024,512]{1,0:T(8,128)(2,1)S(1)}, bf16[1024,512]{1,0:T(8,128)(2,1)S(1)}, u32[]{:S(2)}, u32[]{:S(2)}) collective-permute-start(bf16[1024,512]{1,0:T(8,128)(2,1)S(1)} %collective-permute-done), channel_id=1, source_target_pairs={{0,4},{4,8},{8,12},{12,0},{1,5},{5,9},{9,13},{13,1},{2,6},{6,10},{... | collective-permute-start | bytes 3145736 | tf_op jit(solution)/shard_map/ppermute | solution.py:101
  67.8 39.6 %collective-permute-start.2 = (bf16[1024,512]{1,0:T(8,128)(2,1)S(1)}, bf16[1024,512]{1,0:T(8,128)(2,1)}, u32[]{:S(2)}, u32[]{:S(2)}) collective-permute-start(bf16[1024,512]{1,0:T(8,128)(2,1)S(1)} %collective-permute-done.1), channel_id=1, source_target_pairs={{0,4},{4,8},{8,12},{12,0},{1,5},{5,9},{9,13},{13,1},{2,6},{6,10},{... | collective-permute-start | bytes 3145736 | tf_op jit(solution)/shard_map/ppermute | solution.py:101
  175.2 74.4 %copy-start.3 = (bf16[512,512]{0,1:T(8,128)(2,1)}, bf16[512,512]{0,1:T(8,128)(2,1)S(1)}, u32[]{:S(2)}) copy-start(bf16[512,512]{0,1:T(8,128)(2,1)S(1)} %convolution_convert_fusion) | copy-start | bytes 1572868
  256.4 1.2 copy-start.1
  257.6 19.6 %copy-start.2 = (bf16[512,512]{1,0:T(8,128)(2,1)S(1)}, bf16[512,512]{1,0:T(8,128)(2,1)}, u32[]{:S(2)}) copy-start(bf16[512,512]{1,0:T(8,128)(2,1)} %all_gather.22) | copy-start | bytes 1572868
Sparse Core Ops, SparseCore 0:
  11.5 19.4 all-gather.10
  32.5 34.4 all-gather.4
  68.6 100.7 all-gather.8
  170.8 78.7 all-gather.6
